TPU v7x, 256 devices: a whole 4x4x8 slice. The times are simulated.
256 devices in a mesh: slab: 64 (over x, z, core), img: 4 (over y).
Axes of the slice: x: 4, y: 4, z: 8, core: 2. Of those that a mesh axis runs over, the one named last changes fastest.
Arguments:
- volume: bfloat16 [32768, 256], P('slab'), may hold values from -6 to 6
- interp: bfloat16 [4, 64, 16, 32768], P('img', None, None, 'slab'), may hold values from -0.09375 to 0.09375
- block_index: int32 [4, 64, 64], P('img'), may hold values from 0 to 7
- images: bfloat16 [4, 1024, 128, 256], P('img', 'slab'), may hold values from -6 to 6
- defocus: float32 [4, 1024], P('img', 'slab'), may hold values from 5000 to 25000
- orient: int32 [4, 1024, 4], P('img', 'slab'), may hold values from 0 to 63, all different within a row
Outputs:
- update: float32 [32768, 256], P('slab')
- weights: float32 [4, 1024, 64], P('img', 'slab')
Inputs may be any that keep to these rules, and one draw needn't show every extreme that they name: `orient`: each image lists 4 different orientations of its group.
All inputs are finite; a program needn't handle non-finite values.
Results may differ from a plain program's by a relative error of at most 0.0077.
Values may be sent and summed in bfloat16 or wider, within the bound.
A program may use at most 64 MiB of HBM per device.

v0:
```python
import math
import jax
import jax.numpy as jnp
from jax import lax
from jax.sharding import PartitionSpec as P

BOX = 256
NS = 16
wave_length = 0.0197
aberration = 27000000.0
amplitude = 0.1
grid_side = 4


def phase_tables(fourier, shifts, box):
    freq = (jnp.arange(fourier, dtype=jnp.int32) - fourier // 2).astype(jnp.float32)
    shift_steps = jnp.arange(shifts, dtype=jnp.int32)
    shift_x = (2 * (shift_steps // grid_side) - (grid_side - 1)).astype(jnp.float32)
    shift_y = (2 * (shift_steps % grid_side) - (grid_side - 1)).astype(jnp.float32)
    angle = 2.0 * math.pi / box * (freq[:, None, None] * shift_x + freq[None, :, None] * shift_y)
    forward = jnp.stack([jnp.cos(angle), jnp.sin(angle)], axis=1).reshape(
        2 * fourier * fourier, shifts
    )
    backward = jnp.stack([jnp.cos(angle), -jnp.sin(angle)], axis=1).reshape(
        2 * fourier * fourier, shifts
    )
    return (forward.astype(jnp.bfloat16), backward.T.astype(jnp.bfloat16))


def contrast(defocus_blk, fourier, box):
    freq = (jnp.arange(fourier, dtype=jnp.int32) - fourier // 2).astype(jnp.float32)
    wave_sq = (freq[:, None] * freq[:, None] + freq[None, :] * freq[None, :]) / (box * box)
    phase = math.pi * wave_length * defocus_blk[:, None, None] * wave_sq
    phase = phase - 0.5 * math.pi * aberration * wave_length**3 * wave_sq * wave_sq
    return -(math.sqrt(1.0 - amplitude * amplitude) * jnp.sin(phase) + amplitude * jnp.cos(phase))


def correlate(panels, image_blk, list_blk, defocus_blk, phase_fwd, phase_back, box):
    count = image_blk.shape[0]
    fourier = image_blk.shape[1]
    picks = list_blk.shape[1]
    shifts = phase_fwd.shape[1]
    ctf = contrast(defocus_blk, fourier, box)
    weighted = ctf[:, :, None, :] * image_blk.astype(jnp.float32).reshape(
        count, fourier, 2, fourier
    )
    real_u = weighted[:, None, :, 0]
    imag_u = weighted[:, None, :, 1]
    chosen = panels[list_blk].astype(jnp.float32).reshape(count, picks, fourier, 2, fourier)
    real_p = chosen[:, :, :, 0]
    imag_p = chosen[:, :, :, 1]
    product = jnp.stack(
        [real_p * real_u + imag_p * imag_u, real_p * imag_u - imag_p * real_u], axis=3
    )
    product = product.astype(jnp.bfloat16).reshape(count * picks, 2 * fourier * fourier)
    scores = jnp.dot(product, phase_fwd, preferred_element_type=jnp.float32) / fourier
    scores = scores.reshape(count, picks * shifts)
    squared = scores * scores
    weights = squared / (jnp.mean(squared, axis=1, keepdims=True) + 1e-05)
    rounded = weights.astype(jnp.bfloat16).reshape(count * picks, shifts)
    spread = jnp.dot(rounded, phase_back, preferred_element_type=jnp.float32)
    spread = spread.reshape(count, picks, fourier, 2, fourier)
    real_e = spread[:, :, :, 0]
    imag_e = spread[:, :, :, 1]
    backed = jnp.stack(
        [real_u * real_e - imag_u * imag_e, real_u * imag_e + imag_u * real_e], axis=3
    )
    backed = backed.astype(jnp.bfloat16).reshape(count * picks, 2 * fourier * fourier)
    return (weights, backed)


def on_device(volume, interp, block_index, images, defocus, orient):
    slab_count = lax.axis_size("slab")
    slab_index = lax.axis_index("slab")
    orient_count = interp.shape[1]
    ori_dev = orient_count // slab_count
    block_rows = interp.shape[2]
    fourier = images.shape[2]
    block_count = fourier // block_rows
    img_dev = images.shape[1]
    picks = orient.shape[2]
    levels = jnp.arange(block_count, dtype=jnp.int32)
    partial_value = jnp.einsum("jpr,rx->jpx", interp[0], volume, preferred_element_type=jnp.float32)
    own_blocks = lax.dynamic_index_in_dim(block_index[0], slab_index, axis=1, keepdims=False)
    owned_idx = lax.dynamic_slice_in_dim(block_index[0], slab_index * ori_dev, ori_dev, 0)
    chosen = (own_blocks[:, None] == levels[None, :]).astype(jnp.float32)
    summed = lax.psum_scatter(
        (chosen[:, :, None, None] * partial_value[:, None]).reshape(
            lax.axis_size("slab") * ori_dev, fourier, 2 * fourier
        ),
        "slab",
        scatter_dimension=0,
        tiled=True,
    )
    panels = lax.all_gather(summed.astype(jnp.bfloat16), "slab", axis=0, tiled=True)
    phase_fwd, phase_back = phase_tables(fourier, NS, BOX)
    blk = math.gcd(img_dev, 32)
    blk_total = img_dev // blk

    def per_block(pieces):
        image_blk, list_blk, defocus_blk = pieces
        return correlate(panels, image_blk, list_blk, defocus_blk, phase_fwd, phase_back, BOX)

    weights, backs = lax.map(
        per_block,
        (
            images[0].reshape(blk_total, blk, fourier, 2 * fourier),
            orient[0].reshape(blk_total, blk, picks),
            defocus[0].reshape(blk_total, blk),
        ),
    )
    all_slices = backs.reshape(img_dev * picks, 2 * fourier * fourier)
    member = (
        orient[0].reshape(-1)[:, None] == jnp.arange(orient_count, dtype=jnp.int32)[None, :]
    ).astype(jnp.bfloat16)
    back_own = lax.psum_scatter(
        lax.dot_general(
            member, all_slices, (((0,), (0,)), ((), ())), preferred_element_type=jnp.float32
        ),
        "slab",
        scatter_dimension=0,
        tiled=True,
    ).astype(jnp.bfloat16)
    back_own = back_own.reshape(ori_dev, block_count, block_rows, 2 * fourier)
    chosen_back = (owned_idx[:, :, None] == levels).astype(jnp.bfloat16)
    outgoing = jnp.einsum(
        "osb,obpx->sopx", chosen_back, back_own, preferred_element_type=jnp.float32
    )
    outgoing = outgoing.astype(jnp.bfloat16).reshape(slab_count * ori_dev, block_rows, 2 * fourier)
    incoming = lax.all_to_all(outgoing, "slab", split_axis=0, concat_axis=0, tiled=True)
    column = jnp.einsum("jpr,jpx->rx", interp[0], incoming, preferred_element_type=jnp.float32)
    summed_cols = lax.psum(column, "img")
    update = summed_cols / math.sqrt(img_dev * slab_count)
    return (update, weights)


def solution(mesh):
    return jax.shard_map(
        on_device,
        mesh=mesh,
        in_specs=(
            P("slab", None),
            P("img", None, None, "slab"),
            P("img", None, None),
            P("img", "slab", None, None),
            P("img", "slab"),
            P("img", "slab", None),
        ),
        out_specs=(P("slab", None), P("img", "slab", None)),
        check_vma=False,
    )
```

profile of v0, /device:TPU:2, one launch (start us, length us, event | category | flops | bytes accessed | tf_op | source)
XLA Modules:
  0.0 703.3 jit_solution(17142144156621512723)
XLA Ops:
  8.4 1.4 fusion.7
  9.8 3.9 bitcast_multiply_fusion
  13.7 153.4 %reduce-scatter.2.cloned.1.call-done = f32[1,128,256]{2,1,0:T(8,128)} async-done(((f32[64,128,256]{2,1,0:T(8,128)}), f32[1,128,256]{2,1,0:T(8,128)}) %reduce-scatter.2.cloned.1.call-update) | async-done | bytes 131088 | tf_op jit(solution)/shard_map/reduce_scatter | solution.py:87
  167.2 1.5 convert_element_type.137
  169.1 2.1 reshape.427
  171.4 5.4 fusion.10
  177.6 1.9 copy.58
  179.6 2.6 convert_element_type.143
  183.7 3.9 add_negate_fusion
  187.5 1.2 copy_multiply_fusion
  188.8 1.1 slice_bitcast_fusion.1
  189.9 57.4 %all-gather.2.cloned.1.call-done = bf16[64,128,256]{2,1,0:T(8,128)(2,1)} async-done(((bf16[1,128,256]{2,1,0:T(8,128)(2,1)}), bf16[64,128,256]{2,1,0:T(8,128)(2,1)}) %all-gather.2.cloned.1.call-update) | async-done | bytes 4194320 | tf_op jit(solution)/shard_map/all_gather | solution.py:95
  247.3 4.9 gather_fusion
  252.2 7.0 copy.53
  259.2 7.8 %fusion.30 = (f32[16,4,128,1,128]{2,4,3,1,0:T(8,128)}, f32[16,4,128,1,128]{2,4,3,1,0:T(8,128)}) fusion(f32[16,4,128,2,128]{2,4,3,1,0:T(8,128)} %bitcast.54), kind=kLoop, calls=%fused_computation.71 | loop fusion | bytes 16777216 | tf_op jit(solution)/shard_map/while/body/eval_jaxpr/slice | solution.py:50
  267.0 5.5 copy.73
  272.5 5.5 copy.74
  277.9 4.9 add_convert_fusion.1
  283.2 6.6 copy.56
  289.8 7.8 %convert_element_type.140 = bf16[64,32768]{1,0:T(8,128)(2,1)} reshape(bf16[16,4,128,2,128]{4,3,2,1,0:T(2,128)(2,1)} %copy.56) | data formatting | bytes 8388608 | tf_op jit(solution)/shard_map/while/body/eval_jaxpr/convert_element_type | solution.py:55
  297.6 3.7 fusion.31
  301.9 2.4 fusion.3
  304.2 1.5 subtract_convert_fusion
  306.1 6.5 copy.61
  312.7 7.9 %convert_element_type.145 = bf16[64,32768]{1,0:T(8,128)(2,1)} reshape(bf16[16,4,128,2,128]{4,3,2,1,0:T(2,128)(2,1)} %copy.61) | data formatting | bytes 8388608 | tf_op jit(solution)/shard_map/while/body/eval_jaxpr/convert_element_type | solution.py:68
  320.5 6.8 fusion.15
  327.3 257.5 %all-reduce.5 = bf16[64,32768]{1,0:T(8,128)(2,1)} all-reduce(f32[64,32768]{1,0:T(8,128)} %fusion.15), channel_id=3, replica_groups=mesh['slab'=64,'img'=4] {'slab'}, use_global_device_ids=true, to_apply=%region_3.4.clone | all-reduce | flops 2097152 | bytes 12582912
  584.8 2.1 fusion.12
  587.6 59.8 %all_to_all.5 = bf16[64,16,256]{2,1,0:T(8,128)(2,1)S(1)} all-to-all(bf16[64,16,256]{2,1,0:T(8,128)(2,1)S(1)} %copy.63), channel_id=1, replica_groups=mesh['slab'=64,'img'=4] {'slab'}, dimensions={0} | all-to-all | bytes 1048576 | tf_op jit(solution)/shard_map/all_to_all | solution.py:130
  647.3 1.2 convolution_bitcast_fusion
  649.4 45.2 %all-reduce.4.cloned.1.call-done = f32[512,256]{0,1:T(8,128)} async-done(((f32[512,256]{0,1:T(8,128)}), f32[512,256]{0,1:T(8,128)}) %all-reduce.4.cloned.1.call-update) | async-done | bytes 524304 | tf_op jit(solution)/shard_map/psum | solution.py:132
  694.7 1.1 broadcast_multiply_fusion
  (56 shorter events, 7.9 us)
Async XLA Ops:
  7.2 1.2 copy-start
  7.2 160.0 %reduce-scatter.2.cloned.1.call-start = ((), (), s32[]{:S(2)}) async-start(), calls=%async_computation.2 | async-start | bytes 8519680 | tf_op jit(solution)/shard_map/reduce_scatter | solution.py:87
  13.7 155.1 %copy-start.4 = (s32[1,16,4]{1,2,0:T(4,128)S(1)}, s32[1,16,4]{1,2,0:T(4,128)}, u32[]{:S(2)}) copy-start(s32[1,16,4]{1,2,0:T(4,128)} %param.11) | copy-start | bytes 772
  13.7 233.6 %all-gather.2.cloned.1.call-start = ((), (), s32[]{:S(2)}) async-start(), calls=%async_computation.3 | async-start | bytes 4259840 | tf_op jit(solution)/shard_map/all_gather | solution.py:95
  168.7 525.9 %all-reduce.4.cloned.1.call-start = ((), (), s32[]{:S(2)}) async-start(), calls=%async_computation.4 | async-start | bytes 1048576 | tf_op jit(solution)/shard_map/psum | solution.py:132
  171.1 11.1 %copy-start.6 = (u32[256]{0:T(256)S(1)}, u32[256]{0:T(256)}, u32[]{:S(2)}) copy-start(u32[256]{0:T(256)} %constant.117) | copy-start | bytes 3076
  171.2 12.4 %copy-start.5 = (f32[1,16]{1,0:T(1,128)S(1)}, f32[1,16]{1,0:T(1,128)}, u32[]{:S(2)}) copy-start(f32[1,16]{1,0:T(1,128)} %param.10) | copy-start | bytes 196
  176.7 0.8 copy-start.2
  297.6 4.3 copy-start.3
  301.9 2.4 copy-start.1
Sparse Core Ops, SparseCore 0:
  13.8 153.3 reduce-scatter.1
  170.3 76.9 all-gather.1
  648.7 45.8 all-reduce.3
where the time goes:
time: 704 us; the launch traced here: 703 us
  blocking collectives  317 us (45%)
  waiting for transfers between devices  256 us (36%)
  local copies, waits for them, and re-layouts  74.8 us (11%)
  other arithmetic  25.2 us (4%)
  matrix products  15.8 us (2%)
  between operations  14 us (2%)
    unnamed x1, blocking collectives  257 us
    reduce_scatter x1, waiting for transfers between devices, on_device(): lax.psum_scatter((chosen[:, :, None, None] * partial_value[:, None]).resh...  153 us
    all_to_all x1, blocking collectives, on_device(): lax.all_to_all(outgoing, 'slab', split_axis=0, concat_axis=0, tiled=True)  59.8 us
    all_gather x1, waiting for transfers between devices, on_device(): lax.all_gather(summed.astype(jnp.bfloat16), 'slab', axis=0, tiled=True)  57.4 us
    psum x1, waiting for transfers between devices, on_device(): summed_cols = lax.psum(column, 'img')  45.2 us
  transfers between devices with their start and end apart: 3, of which 3 were waited for; matrix products, arithmetic and copies ran while one was open for 3% of the time, Pallas kernels for 0%

commit v1 on v0

--- a/solution.py
+++ b/solution.py
@@ -92,7 +92,12 @@
         scatter_dimension=0,
         tiled=True,
     )
-    panels = lax.all_gather(summed.astype(jnp.bfloat16), "slab", axis=0, tiled=True)
+    panels = jnp.concatenate(
+        lax.all_to_all(
+            jnp.stack([summed.astype(jnp.bfloat16)] * lax.axis_size("slab")), "slab", 0, 0
+        ),
+        axis=0,
+    )
     phase_fwd, phase_back = phase_tables(fourier, NS, BOX)
     blk = math.gcd(img_dev, 32)
     blk_total = img_dev // blk

time: 704 us -> 729 us (1.036)
  waiting for transfers between devices: 256 us -> 272 us
  starting transfers between devices: 0.12 us -> 8.88 us
    all_to_all x0 -> x1, waiting for transfers between devices: none -> 73.4 us  [on_device(): lax.all_to_all(jnp.stack([summed.astype(jnp.bfloat16)] * lax.axis_size('s...]
    all_gather x1 -> x0, waiting for transfers between devices: 57.4 us -> none  [on_device(): lax.all_gather(summed.astype(jnp.bfloat16), 'slab', axis=0, tiled=True)]
    all_to_all x0 -> x1, starting transfers between devices: none -> 8.61 us  [on_device(): lax.all_to_all(jnp.stack([summed.astype(jnp.bfloat16)] * lax.axis_size('s...]
where the time goes in v1:
time: 729 us; the launch traced here: 728 us
  blocking collectives  315 us (43%)
  waiting for transfers between devices  272 us (37%)
  local copies, waits for them, and re-layouts  77.3 us (11%)
  other arithmetic  24.6 us (3%)
  matrix products  15.8 us (2%)
  between operations  14.3 us (2%)
  starting transfers between devices  8.88 us (1%)
    unnamed x1, blocking collectives  256 us
    reduce_scatter x1, waiting for transfers between devices, on_device(): lax.psum_scatter((chosen[:, :, None, None] * partial_value[:, None]).resh...  153 us
    all_to_all x1, waiting for transfers between devices, on_device(): lax.all_to_all(jnp.stack([summed.astype(jnp.bfloat16)] * lax.axis_size('s...  73.4 us
    all_to_all x1, blocking collectives, on_device(): lax.all_to_all(outgoing, 'slab', split_axis=0, concat_axis=0, tiled=True)  59.3 us
    psum x1, waiting for transfers between devices, on_device(): summed_cols = lax.psum(column, 'img')  45.1 us
  transfers between devices with their start and end apart: 3, of which 3 were waited for; matrix products, arithmetic and copies ran while one was open for 3% of the time, Pallas kernels for 0%

profile of v1, /device:TPU:2, one launch (start us, length us, event | category | flops | bytes accessed | tf_op | source)
XLA Modules:
  0.0 727.9 jit_solution(18114812535091587456)
XLA Ops:
  8.4 1.4 fusion.7
  9.8 3.9 bitcast_multiply_fusion
  13.7 153.5 %reduce-scatter.2.cloned.1.call-done = f32[1,128,256]{2,1,0:T(8,128)} async-done(((f32[64,128,256]{2,1,0:T(8,128)}), f32[1,128,256]{2,1,0:T(8,128)}) %reduce-scatter.2.cloned.1.call-update) | async-done | bytes 131088 | tf_op jit(solution)/shard_map/reduce_scatter | solution.py:87
  168.1 2.5 stack.20
  170.5 8.6 %all-to-all-start = ((bf16[64,1,128,256]{3,2,1,0:T(8,128)(2,1)}), bf16[64,1,128,256]{3,2,1,0:T(8,128)(2,1)}, u32[]{:S(2)}, u32[]{:S(2)}) async-start(bf16[64,1,128,256]{3,2,1,0:T(8,128)(2,1)} %stack.20), calls=%async_computation.1 | async-start | bytes 8388608 | tf_op jit(solution)/shard_map/all_to_all | solution.py:96
  179.7 2.1 reshape.434
  182.0 5.4 fusion.10
  188.3 2.0 copy.58
  190.3 2.6 convert_element_type.146
  194.4 3.9 add_negate_fusion
  198.2 1.2 copy_multiply_fusion
  199.5 1.1 slice_bitcast_fusion.1
  200.6 73.4 %all-to-all-done = bf16[64,1,128,256]{3,2,1,0:T(8,128)(2,1)} async-done(((bf16[64,1,128,256]{3,2,1,0:T(8,128)(2,1)}), bf16[64,1,128,256]{3,2,1,0:T(8,128)(2,1)}, u32[]{:S(2)}, u32[]{:S(2)}) %all-to-all-start) | async-done | bytes 4194336 | tf_op jit(solution)/shard_map/all_to_all | solution.py:96
  274.0 4.9 gather_fusion
  279.0 7.0 copy.53
  286.0 7.8 %fusion.30 = (f32[16,4,128,1,128]{2,4,3,1,0:T(8,128)}, f32[16,4,128,1,128]{2,4,3,1,0:T(8,128)}) fusion(f32[16,4,128,2,128]{2,4,3,1,0:T(8,128)} %bitcast.57), kind=kLoop, calls=%fused_computation.72 | loop fusion | bytes 16777216 | tf_op jit(solution)/shard_map/while/body/eval_jaxpr/slice | solution.py:50
  293.8 5.5 copy.73
  299.2 5.5 copy.74
  304.7 4.9 add_convert_fusion.1
  310.0 6.6 copy.56
  316.6 7.8 %convert_element_type.143 = bf16[64,32768]{1,0:T(8,128)(2,1)} reshape(bf16[16,4,128,2,128]{4,3,2,1,0:T(2,128)(2,1)} %copy.56) | data formatting | bytes 8388608 | tf_op jit(solution)/shard_map/while/body/eval_jaxpr/convert_element_type | solution.py:55
  324.4 3.7 fusion.31
  328.6 2.4 fusion.3
  331.0 1.5 subtract_convert_fusion
  332.9 6.6 copy.61
  339.5 7.8 %convert_element_type.148 = bf16[64,32768]{1,0:T(8,128)(2,1)} reshape(bf16[16,4,128,2,128]{4,3,2,1,0:T(2,128)(2,1)} %copy.61) | data formatting | bytes 8388608 | tf_op jit(solution)/shard_map/while/body/eval_jaxpr/convert_element_type | solution.py:68
  347.3 6.8 fusion.15
  354.1 255.6 %all-reduce.5 = bf16[64,32768]{1,0:T(8,128)(2,1)} all-reduce(f32[64,32768]{1,0:T(8,128)} %fusion.15), channel_id=3, replica_groups=mesh['slab'=64,'img'=4] {'slab'}, use_global_device_ids=true, to_apply=%region_3.4.clone | all-reduce | flops 2097152 | bytes 12582912
  609.6 2.1 fusion.12
  612.4 59.3 %all_to_all.10 = bf16[64,16,256]{2,1,0:T(8,128)(2,1)S(1)} all-to-all(bf16[64,16,256]{2,1,0:T(8,128)(2,1)S(1)} %copy.63), channel_id=1, replica_groups=mesh['slab'=64,'img'=4] {'slab'}, dimensions={0} | all-to-all | bytes 1048576 | tf_op jit(solution)/shard_map/all_to_all | solution.py:135
  671.8 1.2 convolution_bitcast_fusion
  673.9 45.1 %all-reduce.4.cloned.1.call-done = f32[512,256]{0,1:T(8,128)} async-done(((f32[512,256]{0,1:T(8,128)}), f32[512,256]{0,1:T(8,128)}) %all-reduce.4.cloned.1.call-update) | async-done | bytes 524304 | tf_op jit(solution)/shard_map/psum | solution.py:137
  (56 shorter events, 10.0 us)
Async XLA Ops:
  7.2 1.2 copy-start
  7.2 160.0 %reduce-scatter.2.cloned.1.call-start = ((), (), s32[]{:S(2)}) async-start(), calls=%async_computation.3 | async-start | bytes 8519680 | tf_op jit(solution)/shard_map/reduce_scatter | solution.py:87
  170.5 8.9 %copy-start.4 = (s32[1,16,4]{1,2,0:T(4,128)S(1)}, s32[1,16,4]{1,2,0:T(4,128)}, u32[]{:S(2)}) copy-start(s32[1,16,4]{1,2,0:T(4,128)} %param.11) | copy-start | bytes 772
  170.5 103.5 %all-to-all-start = ((bf16[64,1,128,256]{3,2,1,0:T(8,128)(2,1)}), bf16[64,1,128,256]{3,2,1,0:T(8,128)(2,1)}, u32[]{:S(2)}, u32[]{:S(2)}) async-start(bf16[64,1,128,256]{3,2,1,0:T(8,128)(2,1)} %stack.20), calls=%async_computation.1 | async-start | bytes 8388608 | tf_op jit(solution)/shard_map/all_to_all | solution.py:96
  179.2 539.8 %all-reduce.4.cloned.1.call-start = ((), (), s32[]{:S(2)}) async-start(), calls=%async_computation.4 | async-start | bytes 1048576 | tf_op jit(solution)/shard_map/psum | solution.py:137
  181.8 11.2 %copy-start.6 = (u32[256]{0:T(256)S(1)}, u32[256]{0:T(256)}, u32[]{:S(2)}) copy-start(u32[256]{0:T(256)} %constant.117) | copy-start | bytes 3076
  181.8 12.5 %copy-start.5 = (f32[1,16]{1,0:T(1,128)S(1)}, f32[1,16]{1,0:T(1,128)}, u32[]{:S(2)}) copy-start(f32[1,16]{1,0:T(1,128)} %param.10) | copy-start | bytes 196
  187.4 0.8 copy-start.2
  324.4 4.3 copy-start.3
  328.6 2.4 copy-start.1
Sparse Core Ops, SparseCore 0:
  13.8 153.3 reduce-scatter.1
  673.1 45.7 all-reduce.3
